TPU v7x, 32 devices: a whole 2x2x4 slice. The times are simulated.
32 devices in a mesh: dp: 8 (over z, y), tensor: 4 (over x, core).
Axes of the slice: x: 2, y: 2, z: 4, core: 2. Of those that a mesh axis runs over, the one named last changes fastest.
Arguments:
- inputs: bfloat16 [608, 8, 1024], P('tensor', 'dp'), may hold values from -6 to 6
- attn_gain: bfloat16 [2, 1024], P(None, 'dp'), may hold values from 0.5 to 1.5
- attn_shift: bfloat16 [2, 1024], P(None, 'dp'), may hold values from -1.25 to 1.25
- qkv_weight: bfloat16 [2, 1024, 3, 1024], P(None, 'dp', None, 'tensor'), may hold values from -0.1875 to 0.1875
- query_bias: bfloat16 [2, 1024], P(None, 'dp'), may hold values from -3 to 3
- value_bias: bfloat16 [2, 1024], P(None, 'dp'), may hold values from -1.25 to 1.25
- out_weight: bfloat16 [2, 1024, 1024], P(None, 'tensor', 'dp'), may hold values from -2 to 2
- out_bias: bfloat16 [2, 1024], P(None, 'dp'), may hold values from -1.25 to 1.25
- mlp_gain: bfloat16 [2, 1024], P(None, 'dp'), may hold values from 0.5 to 1.5
- mlp_shift: bfloat16 [2, 1024], P(None, 'dp'), may hold values from -1.25 to 1.25
- up_weight: bfloat16 [2, 1024, 4096], P(None, 'dp', 'tensor'), may hold values from -0.1875 to 0.1875
- up_bias: bfloat16 [2, 4096], P(None, 'dp'), may hold values from -1.25 to 1.25
- down_weight: bfloat16 [2, 4096, 1024], P(None, 'tensor', 'dp'), may hold values from -0.09375 to 0.09375
- down_bias: bfloat16 [2, 1024], P(None, 'dp'), may hold values from -1.25 to 1.25
- cotangent: bfloat16 [608, 8, 1024], P('tensor', 'dp'), may hold values from -6 to 6
- image_mask: int32 [8], P('dp'), may hold values 0 or 1
- row_mask: int32 [608, 8], P(None, 'dp'), may hold values from 0 to 1, as said below
Outputs:
- outputs: bfloat16 [608, 8, 1024], P('tensor', 'dp')
- grad_inputs: float32 [608, 8, 1024], P('tensor', 'dp')
- grad_attn_gain: float32 [2, 1024], P(None, 'dp')
- grad_attn_shift: float32 [2, 1024], P(None, 'dp')
- grad_qkv_weight: float32 [2, 1024, 3, 1024], P(None, 'dp', None, 'tensor')
- grad_query_bias: float32 [2, 1024], P(None, 'dp')
- grad_value_bias: float32 [2, 1024], P(None, 'dp')
- grad_out_weight: float32 [2, 1024, 1024], P(None, 'tensor', 'dp')
- grad_out_bias: float32 [2, 1024], P(None, 'dp')
- grad_mlp_gain: float32 [2, 1024], P(None, 'dp')
- grad_mlp_shift: float32 [2, 1024], P(None, 'dp')
- grad_up_weight: float32 [2, 1024, 4096], P(None, 'dp', 'tensor')
- grad_up_bias: float32 [2, 4096], P(None, 'dp')
- grad_down_weight: float32 [2, 4096, 1024], P(None, 'tensor', 'dp')
- grad_down_bias: float32 [2, 1024], P(None, 'dp')
Inputs may be any that keep to these rules, and one draw needn't show every extreme that they name: `row_mask`: row 0 of every image is live; rows 577 and later are 0.
All inputs are finite; a program needn't handle non-finite values. No bound on the sum of `image_mask` on one device may be relied on, other than what follows from the above.
Results may differ from a plain program's by a relative error of at most 0.015.
Values may be sent and summed in bfloat16 or wider, within the bound.
A program may use at most 128 MiB of HBM per device.

v0:
```python
import jax
import jax.numpy as jnp
from jax import lax
from jax.sharding import PartitionSpec as P

HEAD_DIM = 64


def layer_norm(values, gain, shift):
    center = values - jnp.mean(values, -1, keepdims=True)
    inverse = lax.rsqrt(jnp.mean(center * center, -1, keepdims=True) + 1e-05)
    return center * inverse * gain + shift


def norm_backward(values, gain, grad_out):
    center = values - jnp.mean(values, -1, keepdims=True)
    inverse = lax.rsqrt(jnp.mean(center * center, -1, keepdims=True) + 1e-05)
    normal = center * inverse
    grad_hat = grad_out * gain
    grad_in = inverse * (
        grad_hat
        - jnp.mean(grad_hat, -1, keepdims=True)
        - normal * jnp.mean(grad_hat * normal, -1, keepdims=True)
    )
    return (grad_in, jnp.sum(grad_out * normal, (0, 1)), jnp.sum(grad_out, (0, 1)))


def quick_gelu(values):
    return values * jax.nn.sigmoid(1.702 * values)


def gelu_slope(values):
    sigma = jax.nn.sigmoid(1.702 * values)
    return sigma + 1.702 * values * sigma * (1.0 - sigma)


def image_scores(block, keep):
    scores = jnp.einsum(
        "qhe,khe->hqk", block[:, 0], block[:, 1], preferred_element_type=jnp.float32
    )
    scores = scores * HEAD_DIM ** (-0.5)
    return jnp.where(keep[None, None, :], scores, -1e30)


def attention_forward(qkv, row_mask):
    seq_len, images, width = (qkv.shape[0], qkv.shape[1], qkv.shape[3])
    heads = width // HEAD_DIM

    def one_image(which, carry):
        outs, lses = carry
        block = lax.dynamic_index_in_dim(qkv, which, 1, keepdims=False).reshape(
            seq_len, 3, heads, HEAD_DIM
        )
        keep = lax.dynamic_index_in_dim(row_mask, which, 1, keepdims=False) > 0
        scores = image_scores(block, keep)
        row_max = jnp.max(scores, -1, keepdims=True)
        expo = jnp.exp(scores - row_max)
        row_total = jnp.sum(expo, -1, keepdims=True)
        weights = (expo / row_total).astype(jnp.bfloat16)
        values = jnp.einsum(
            "hqk,khe->qhe", weights, block[:, 2], preferred_element_type=jnp.float32
        )
        values = values.astype(jnp.bfloat16).reshape(seq_len, 1, width)
        outs = values
        lses = lax.dynamic_update_index_in_dim(
            lses, (row_max + jnp.log(row_total))[:, :, 0], which, 0
        )
        return (outs, lses)

    start = (
        jnp.zeros((seq_len, images, width), jnp.bfloat16),
        jnp.zeros((images, heads, seq_len), jnp.float32),
    )
    return lax.fori_loop(0, images, one_image, start)


def attention_backward(qkv, lses, grad_mixed, row_mask):
    seq_len, images, width = (qkv.shape[0], qkv.shape[1], qkv.shape[3])
    heads = width // HEAD_DIM
    scale = HEAD_DIM ** (-0.5)

    def one_image(which, grads):
        block = lax.dynamic_index_in_dim(qkv, which, 1, keepdims=False).reshape(
            seq_len, 3, heads, HEAD_DIM
        )
        keep = lax.dynamic_index_in_dim(row_mask, which, 1, keepdims=False) > 0
        grad_out = lax.dynamic_index_in_dim(grad_mixed, which, 1, keepdims=False).reshape(
            seq_len, heads, HEAD_DIM
        )
        lse_here = lax.dynamic_index_in_dim(lses, which, 0, keepdims=False)
        weights = jnp.exp(image_scores(block, keep) - lse_here[:, :, None])
        grad_value = jnp.einsum(
            "hqk,qhe->khe",
            weights.astype(jnp.bfloat16),
            grad_out,
            preferred_element_type=jnp.float32,
        )
        grad_weights = jnp.einsum(
            "qhe,khe->hqk", grad_out, block[:, 2], preferred_element_type=jnp.float32
        )
        delta = jnp.sum(weights * grad_weights, -1, keepdims=True)
        grad_scores = (weights * (grad_weights - delta)).astype(jnp.bfloat16)
        grad_query = (
            jnp.einsum("hqk,khe->qhe", grad_scores, block[:, 1], preferred_element_type=jnp.float32)
            * scale
        )
        grad_key = (
            jnp.einsum("hqk,qhe->khe", grad_scores, block[:, 0], preferred_element_type=jnp.float32)
            * scale
        )
        stacked = jnp.stack([grad_query, grad_key, grad_value], 1).astype(jnp.bfloat16)
        return stacked.reshape(seq_len, 1, 3, width)

    return lax.fori_loop(0, images, one_image, jnp.zeros(qkv.shape, jnp.bfloat16))


def body(
    inputs,
    attn_gain,
    attn_shift,
    qkv_weight,
    query_bias,
    value_bias,
    out_weight,
    out_bias,
    mlp_gain,
    mlp_shift,
    up_weight,
    up_bias,
    down_weight,
    down_bias,
    cotangent,
    image_mask,
    row_mask,
):
    depth_count = qkv_weight.shape[0]
    tensor_rank = lax.axis_index("tensor")
    local_rows = inputs.shape[0]
    head_width = qkv_weight.shape[3]
    unit_width = up_weight.shape[2]
    vectors = jnp.stack(
        [attn_gain, attn_shift, query_bias, value_bias, out_bias, mlp_gain, mlp_shift, down_bias], 1
    )

    def fetch(depth):
        return (
            lax.all_gather(qkv_weight[depth], "dp", axis=0, tiled=True),
            lax.all_gather(up_weight[depth], "dp", axis=0, tiled=True),
            lax.all_gather(out_weight[depth], "dp", axis=1, tiled=True),
            lax.all_gather(down_weight[depth], "dp", axis=1, tiled=True),
            lax.all_gather(vectors[depth], "dp", axis=1, tiled=True),
            lax.all_gather(up_bias[depth], "dp", axis=0, tiled=True),
        )

    def unpack(weights):
        vec = weights[4].astype(jnp.float32)
        query_cols = lax.dynamic_slice_in_dim(vec[2], tensor_rank * head_width, head_width)
        value_cols = lax.dynamic_slice_in_dim(vec[3], tensor_rank * head_width, head_width)
        bias_three = jnp.stack([query_cols, jnp.zeros_like(query_cols), value_cols])
        up_cols = lax.dynamic_slice_in_dim(
            weights[5].astype(jnp.float32), tensor_rank * unit_width, unit_width
        )
        return (vec, bias_three, up_cols)

    def forward_parts(hidden, weights):
        qkv_w, up_w, out_w = (weights[0], weights[1], weights[2])
        vec, bias_three, up_cols = unpack(weights)
        normed = layer_norm(hidden, vec[0], vec[1]).astype(jnp.bfloat16)
        product = jnp.einsum(
            "sid,dce->sice",
            lax.all_gather(normed, "tensor", axis=0, tiled=True),
            qkv_w,
            preferred_element_type=jnp.float32,
        )
        qkv = (product + bias_three).astype(jnp.bfloat16)
        mixed, lses = attention_forward(qkv, row_mask)
        middle = (
            hidden
            + lax.psum_scatter(
                jnp.einsum("sie,ed->sid", mixed, out_w, preferred_element_type=jnp.float32).astype(
                    jnp.bfloat16
                ),
                "tensor",
                scatter_dimension=0,
                tiled=True,
            ).astype(jnp.float32)
            + vec[4]
        )
        normed_mid = layer_norm(middle, vec[5], vec[6]).astype(jnp.bfloat16)
        before = (
            jnp.einsum(
                "sid,df->sif",
                lax.all_gather(normed_mid, "tensor", axis=0, tiled=True),
                up_w,
                preferred_element_type=jnp.float32,
            )
            + up_cols
        )
        active = quick_gelu(before).astype(jnp.bfloat16)
        return (normed, qkv, mixed, lses, middle, normed_mid, before, active)

    hidden = inputs.astype(jnp.float32)
    kept = []
    layer_inputs = []
    stored = []
    for depth in range(depth_count):
        weights = fetch(depth)
        kept.append(weights)
        layer_inputs.append(hidden)
        parts = forward_parts(hidden, weights)
        stored.append(parts)
        down_cols = weights[4][7].astype(jnp.float32)
        mlp_active = parts[7]
        mlp_down_w = weights[3]
        hidden = (
            parts[4]
            + lax.psum_scatter(
                jnp.einsum(
                    "sif,fd->sid", mlp_active, mlp_down_w, preferred_element_type=jnp.float32
                ).astype(jnp.bfloat16),
                "tensor",
                scatter_dimension=0,
                tiled=True,
            ).astype(jnp.float32)
            + down_cols
        )
    live_rows = lax.dynamic_slice_in_dim(row_mask, tensor_rank * local_rows, local_rows, 0)
    live = (live_rows * image_mask[None, :]).astype(jnp.float32)
    grad = cotangent.astype(jnp.float32) * live[:, :, None]
    per_layer = []
    for depth in reversed(range(depth_count)):
        weights = fetch(depth)
        parts = forward_parts(layer_inputs[depth], weights)
        layer_qkv_w = weights[0]
        layer_up_w = weights[1]
        layer_out_w = weights[2]
        down_w = weights[3]
        layer_vec, layer_bias_three, layer_up_cols = unpack(weights)
        (
            layer_normed,
            layer_qkv,
            layer_mixed,
            layer_lses,
            layer_middle,
            layer_normed_mid,
            layer_before,
            layer_active,
        ) = parts
        full_width = layer_vec.shape[1]
        grad_down_bias = jnp.sum(grad, (0, 1))
        fold_piece = lax.all_gather(grad.astype(jnp.bfloat16), "tensor", axis=0, tiled=True)
        update = jnp.einsum("sid,fd->sif", fold_piece, down_w, preferred_element_type=jnp.float32)
        grad_down_w = jnp.einsum(
            "sif,sid->fd", layer_active, fold_piece, preferred_element_type=jnp.float32
        )
        grad_before = (update * gelu_slope(layer_before)).astype(jnp.bfloat16)
        grad_up_cols = jnp.sum(grad_before.astype(jnp.float32), (0, 1))
        grad_up_w = jnp.einsum(
            "sid,sif->df",
            lax.all_gather(layer_normed_mid, "tensor", axis=0, tiled=True),
            grad_before,
            preferred_element_type=jnp.float32,
        )
        grad_normed_mid = lax.psum_scatter(
            jnp.einsum(
                "sif,df->sid", grad_before, layer_up_w, preferred_element_type=jnp.float32
            ).astype(jnp.bfloat16),
            "tensor",
            scatter_dimension=0,
            tiled=True,
        ).astype(jnp.float32)
        grad_mid, grad_mlp_gain, grad_mlp_shift = norm_backward(
            layer_middle, layer_vec[5], grad_normed_mid
        )
        grad_mid = grad_mid + grad
        grad_out_bias = jnp.sum(grad_mid, (0, 1))
        piece = lax.all_gather(grad_mid.astype(jnp.bfloat16), "tensor", axis=0, tiled=True)
        fold_update = jnp.einsum(
            "sid,ed->sie", piece, layer_out_w, preferred_element_type=jnp.float32
        )
        grad_out_w = jnp.einsum(
            "sie,sid->ed", layer_mixed, piece, preferred_element_type=jnp.float32
        )
        grad_qkv = attention_backward(
            layer_qkv, layer_lses, fold_update.astype(jnp.bfloat16), row_mask
        )
        grad_bias_three = jnp.sum(grad_qkv.astype(jnp.float32), (0, 1))
        grad_qkv_w = jnp.einsum(
            "sid,sice->dce",
            lax.all_gather(layer_normed, "tensor", axis=0, tiled=True),
            grad_qkv,
            preferred_element_type=jnp.float32,
        )
        grad_normed = lax.psum_scatter(
            jnp.einsum(
                "sice,dce->sid", grad_qkv, layer_qkv_w, preferred_element_type=jnp.float32
            ).astype(jnp.bfloat16),
            "tensor",
            scatter_dimension=0,
            tiled=True,
        ).astype(jnp.float32)
        grad_in, grad_attn_gain, grad_attn_shift = norm_backward(
            layer_inputs[depth], layer_vec[0], grad_normed
        )
        grad_in = grad_in + grad_mid
        empty = jnp.zeros((full_width,), jnp.float32)
        grad_query = lax.dynamic_update_slice_in_dim(
            empty, grad_bias_three[0], tensor_rank * head_width, 0
        )
        grad_value = lax.dynamic_update_slice_in_dim(
            empty, grad_bias_three[2], tensor_rank * head_width, 0
        )
        grad_up_full = lax.dynamic_update_slice_in_dim(
            jnp.zeros((weights[5].shape[0],), jnp.float32),
            grad_up_cols,
            tensor_rank * unit_width,
            0,
        )
        grad_vec = jnp.stack(
            [
                grad_attn_gain,
                grad_attn_shift,
                grad_query,
                grad_value,
                grad_out_bias,
                grad_mlp_gain,
                grad_mlp_shift,
                grad_down_bias,
            ]
        )
        shards = (
            lax.psum_scatter(grad_qkv_w, "dp", scatter_dimension=0, tiled=True),
            lax.psum_scatter(grad_up_w, "dp", scatter_dimension=0, tiled=True),
            lax.psum_scatter(grad_out_w, "dp", scatter_dimension=1, tiled=True),
            lax.psum_scatter(grad_down_w, "dp", scatter_dimension=1, tiled=True),
            lax.psum_scatter(grad_vec, "dp", scatter_dimension=1, tiled=True),
            lax.psum_scatter(grad_up_full, "dp", scatter_dimension=0, tiled=True),
        )
        grad, shards = (grad_in, shards)
        per_layer.insert(0, shards)
    vec_grads = jnp.stack([shards[4] for shards in per_layer])
    bias_grads = jnp.stack([shards[5] for shards in per_layer])
    vec_sum, up_sum = lax.psum((vec_grads, bias_grads), "tensor")
    return (
        hidden.astype(jnp.bfloat16),
        grad,
        vec_sum[:, 0],
        vec_sum[:, 1],
        jnp.stack([shards[0] for shards in per_layer]),
        vec_sum[:, 2],
        vec_sum[:, 3],
        jnp.stack([shards[2] for shards in per_layer]),
        vec_sum[:, 4],
        vec_sum[:, 5],
        vec_sum[:, 6],
        jnp.stack([shards[1] for shards in per_layer]),
        up_sum,
        jnp.stack([shards[3] for shards in per_layer]),
        vec_sum[:, 7],
    )


def solution(mesh):
    in_specs = (
        P("tensor", "dp", None),
        P(None, "dp"),
        P(None, "dp"),
        P(None, "dp", None, "tensor"),
        P(None, "dp"),
        P(None, "dp"),
        P(None, "tensor", "dp"),
        P(None, "dp"),
        P(None, "dp"),
        P(None, "dp"),
        P(None, "dp", "tensor"),
        P(None, "dp"),
        P(None, "tensor", "dp"),
        P(None, "dp"),
        P("tensor", "dp", None),
        P("dp"),
        P(None, "dp"),
    )
    out_specs = (
        P("tensor", "dp", None),
        P("tensor", "dp", None),
        P(None, "dp"),
        P(None, "dp"),
        P(None, "dp", None, "tensor"),
        P(None, "dp"),
        P(None, "dp"),
        P(None, "tensor", "dp"),
        P(None, "dp"),
        P(None, "dp"),
        P(None, "dp"),
        P(None, "dp", "tensor"),
        P(None, "dp"),
        P(None, "tensor", "dp"),
        P(None, "dp"),
    )
    return jax.shard_map(body, mesh=mesh, in_specs=in_specs, out_specs=out_specs, check_vma=False)
```

profile of v0, /device:TPU:0, one launch (start us, length us, event | category | flops | bytes accessed | tf_op | source)
XLA Modules:
  0.0 1578.2 jit_solution(11736033393084943452)
XLA Ops:
  14.9 22.4 %all-gather = bf16[1,8,1024]{2,0,1:T(2,128)(2,1)S(1)} all-gather(bf16[1,8,128]{2,0,1:T(2,128)(2,1)S(1)} %get-tuple-element.224), channel_id=2, replica_groups=mesh['dp'=8,'tensor'=4] {'dp'}, dimensions={2}, use_global_device_ids=true | all-gather | bytes 18432 | tf_op jit(solution)/shard_map/all_gather | solution.py:151
  58.0 28.1 %all-gather.2 = bf16[1,256,1024]{2,1,0:T(8,128)(2,1)S(1)} all-gather(bf16[1,256,128]{2,1,0:T(8,128)(2,1)S(1)} %get-tuple-element.201), channel_id=4, replica_groups=mesh['dp'=8,'tensor'=4] {'dp'}, dimensions={2}, use_global_device_ids=true | all-gather | bytes 589824 | tf_op jit(solution)/shard_map/all_gather | solution.py:149
  115.2 24.1 %reduce-scatter.19.cloned.1.call-done = bf16[152,1,1024]{2,0,1:T(8,128)(2,1)} async-done(((bf16[608,1,1024]{2,0,1:T(8,128)(2,1)}), bf16[152,1,1024]{2,0,1:T(8,128)(2,1)}) %reduce-scatter.19.cloned.1.call-update) | async-done | bytes 311312 | tf_op jit(solution)/shard_map/reduce_scatter | solution.py:179
  144.7 26.2 %all-gather.4 = bf16[1,4096]{1,0:T(2,128)(2,1)S(1)} all-gather(bf16[1,512]{1,0:T(2,128)(2,1)S(1)} %get-tuple-element.227), channel_id=6, replica_groups=mesh['dp'=8,'tensor'=4] {'dp'}, dimensions={1}, use_global_device_ids=true | all-gather | bytes 9216 | tf_op jit(solution)/shard_map/all_gather | solution.py:152
  214.8 48.9 %all-gather.47.cloned.1.call-done = bf16[1,1024,1024]{2,1,0:T(8,128)(2,1)} async-done(((bf16[1,1024,128]{2,1,0:T(8,128)(2,1)}), bf16[1,1024,1024]{2,1,0:T(8,128)(2,1)}) %all-gather.47.cloned.1.call-update) | async-done | bytes 2097168 | tf_op jit(solution)/shard_map/all_gather | solution.py:150
  269.5 23.6 %reduce-scatter.21.cloned.1.call-done = bf16[152,1,1024]{2,0,1:T(8,128)(2,1)} async-done(((bf16[608,1,1024]{2,0,1:T(8,128)(2,1)}), bf16[152,1,1024]{2,0,1:T(8,128)(2,1)}) %reduce-scatter.21.cloned.1.call-update) | async-done | bytes 311312 | tf_op jit(solution)/shard_map/reduce_scatter | solution.py:217
  295.5 30.9 %all-gather.8 = bf16[1,256,1024]{2,1,0:T(8,128)(2,1)} all-gather(bf16[1,256,128]{2,1,0:T(8,128)(2,1)S(1)} %get-tuple-element.200), channel_id=10, replica_groups=mesh['dp'=8,'tensor'=4] {'dp'}, dimensions={2}, use_global_device_ids=true | all-gather | bytes 589824 | tf_op jit(solution)/shard_map/all_gather | solution.py:149
  374.6 25.5 %reduce-scatter.23.cloned.1.call-done = bf16[152,1,1024]{2,0,1:T(8,128)(2,1)} async-done(((bf16[608,1,1024]{2,0,1:T(8,128)(2,1)}), bf16[152,1,1024]{2,0,1:T(8,128)(2,1)}) %reduce-scatter.23.cloned.1.call-update) | async-done | bytes 311312 | tf_op jit(solution)/shard_map/reduce_scatter | solution.py:179
  404.7 26.2 %all-gather.10 = bf16[1,4096]{1,0:T(2,128)(2,1)S(1)} all-gather(bf16[1,512]{1,0:T(2,128)(2,1)S(1)} %get-tuple-element.226), channel_id=12, replica_groups=mesh['dp'=8,'tensor'=4] {'dp'}, dimensions={1}, use_global_device_ids=true | all-gather | bytes 9216 | tf_op jit(solution)/shard_map/all_gather | solution.py:152
  430.9 21.5 %all-gather.51.cloned.1.call-done = bf16[1,1024,1024]{2,1,0:T(8,128)(2,1)} async-done(((bf16[1,128,1024]{2,1,0:T(8,128)(2,1)}), bf16[1,1024,1024]{2,1,0:T(8,128)(2,1)}) %all-gather.51.cloned.1.call-update) | async-done | bytes 2097168 | tf_op jit(solution)/shard_map/all_gather | solution.py:148
  490.9 53.2 %all-gather.53.cloned.1.call-done = bf16[1,1024,1024]{2,1,0:T(8,128)(2,1)} async-done(((bf16[1,1024,128]{2,1,0:T(8,128)(2,1)}), bf16[1,1024,1024]{2,1,0:T(8,128)(2,1)}) %all-gather.53.cloned.1.call-update) | async-done | bytes 2097168 | tf_op jit(solution)/shard_map/all_gather | solution.py:150
  579.8 26.6 %reduce-scatter.25.cloned.1.call-done = bf16[152,1,1024]{2,0,1:T(8,128)(2,1)} async-done(((bf16[608,1,1024]{2,0,1:T(8,128)(2,1)}), bf16[152,1,1024]{2,0,1:T(8,128)(2,1)}) %reduce-scatter.25.cloned.1.call-update) | async-done | bytes 311312 | tf_op jit(solution)/shard_map/reduce_scatter | solution.py:217
  651.1 26.2 %reduce-scatter.29.cloned.1.call-done = bf16[152,1,1024]{2,0,1:T(8,128)(2,1)} async-done(((bf16[608,1,1024]{2,0,1:T(8,128)(2,1)}), bf16[152,1,1024]{2,0,1:T(8,128)(2,1)}) %reduce-scatter.29.cloned.1.call-update) | async-done | bytes 311312 | tf_op jit(solution)/shard_map/reduce_scatter | solution.py:294
  708.1 25.8 %reduce-scatter.31.cloned.1.call-done = bf16[152,1,1024]{2,0,1:T(8,128)(2,1)} async-done(((bf16[608,1,1024]{2,0,1:T(8,128)(2,1)}), bf16[152,1,1024]{2,0,1:T(8,128)(2,1)}) %reduce-scatter.31.cloned.1.call-update) | async-done | bytes 311312 | tf_op jit(solution)/shard_map/reduce_scatter | solution.py:264
  840.4 37.1 %all-reduce.2 = (f32[4096]{0:T(1024)S(1)}, f32[4096]{0:T(1024)S(1)}) all-reduce(f32[4096]{0:T(1024)S(1)} %dynamic_update_slice.32, f32[4096]{0:T(1024)S(1)} %dynamic_update_slice.31), channel_id=31, replica_groups=mesh['dp'=8,'tensor'=4] {'dp'}, use_global_device_ids=true, to_apply=%region_56.57.clone | all-reduce | flops 8192 | bytes 65536
  877.7 58.1 %reduce-scatter.43.cloned.1.call-done = f32[256,128]{1,0:T(8,128)} async-done(((f32[256,1024]{1,0:T(8,128)}), f32[256,128]{1,0:T(8,128)}) %reduce-scatter.43.cloned.1.call-update) | async-done | bytes 131088 | tf_op jit(solution)/shard_map/reduce_scatter | solution.py:334
  939.2 52.2 %reduce-scatter.37.cloned.1.call-done = f32[8,128]{1,0:T(8,128)} async-done(((f32[8,1024]{1,0:T(8,128)}), f32[8,128]{1,0:T(8,128)}) %reduce-scatter.37.cloned.1.call-update) | async-done | bytes 4112 | tf_op jit(solution)/shard_map/reduce_scatter | solution.py:336
  991.4 55.6 %reduce-scatter.35.cloned.1.call-done = f32[8,128]{1,0:T(8,128)} async-done(((f32[8,1024]{1,0:T(8,128)}), f32[8,128]{1,0:T(8,128)}) %reduce-scatter.35.cloned.1.call-update) | async-done | bytes 4112 | tf_op jit(solution)/shard_map/reduce_scatter | solution.py:336
  1059.0 79.0 %reduce-scatter.53.cloned.1.call-done = f32[1024,128]{1,0:T(8,128)} async-done(((f32[1024,1024]{1,0:T(8,128)}), f32[1024,128]{1,0:T(8,128)}) %reduce-scatter.53.cloned.1.call-update) | async-done | bytes 524304 | tf_op jit(solution)/shard_map/reduce_scatter | solution.py:335
  1138.0 92.3 %reduce-scatter.51.cloned.1.call-done = f32[1024,128]{1,0:T(8,128)} async-done(((f32[1024,1024]{1,0:T(8,128)}), f32[1024,128]{1,0:T(8,128)}) %reduce-scatter.51.cloned.1.call-update) | async-done | bytes 524304 | tf_op jit(solution)/shard_map/reduce_scatter | solution.py:335
  1232.6 89.2 %reduce-scatter.49.cloned.1.call-done = f32[128,1024]{1,0:T(8,128)} async-done(((f32[1024,1024]{1,0:T(8,128)}), f32[128,1024]{1,0:T(8,128)}) %reduce-scatter.49.cloned.1.call-update) | async-done | bytes 524304 | tf_op jit(solution)/shard_map/reduce_scatter | solution.py:333
  1321.8 91.8 %reduce-scatter.47.cloned.1.call-done = f32[128,1024]{1,0:T(8,128)} async-done(((f32[1024,1024]{1,0:T(8,128)}), f32[128,1024]{1,0:T(8,128)}) %reduce-scatter.47.cloned.1.call-update) | async-done | bytes 524304 | tf_op jit(solution)/shard_map/reduce_scatter | solution.py:333
  1415.9 75.9 %reduce-scatter.41.cloned.1.call-done = f32[128,3,256]{2,0,1:T(8,128)} async-done(((f32[1024,3,256]{2,0,1:T(8,128)}), f32[128,3,256]{2,0,1:T(8,128)}) %reduce-scatter.41.cloned.1.call-update) | async-done | bytes 393232 | tf_op jit(solution)/shard_map/reduce_scatter | solution.py:332
  1491.8 77.7 %reduce-scatter.39.cloned.1.call-done = f32[128,3,256]{2,0,1:T(8,128)} async-done(((f32[1024,3,256]{2,0,1:T(8,128)}), f32[128,3,256]{2,0,1:T(8,128)}) %reduce-scatter.39.cloned.1.call-update) | async-done | bytes 393232 | tf_op jit(solution)/shard_map/reduce_scatter | solution.py:332
  (409 shorter events, 443.2 us)
Async XLA Ops:
  7.2 79.0 %all-gather.27.cloned.1.call-start = ((), (), s32[]{:S(2)}) async-start(), calls=%async_computation.18 | async-start | bytes 1556480 | tf_op jit(solution)/shard_map/all_gather | solution.py:171
  41.2 98.2 %reduce-scatter.19.cloned.1.call-start = ((), (), s32[]{:S(2)}) async-start(), calls=%async_computation.19 | async-start | bytes 1556480 | tf_op jit(solution)/shard_map/reduce_scatter | solution.py:179
  114.3 77.2 %all-gather.45.cloned.1.call-start = ((), (), s32[]{:S(2)}) async-start(), calls=%async_computation.45 | async-start | bytes 2359296 | tf_op jit(solution)/shard_map/all_gather | solution.py:148
  115.2 94.7 %all-gather.29.cloned.1.call-start = ((), (), s32[]{:S(2)}) async-start(), calls=%async_computation.20 | async-start | bytes 1556480 | tf_op jit(solution)/shard_map/all_gather | solution.py:193
  143.7 120.0 %all-gather.47.cloned.1.call-start = ((), (), s32[]{:S(2)}) async-start(), calls=%async_computation.46 | async-start | bytes 2359296 | tf_op jit(solution)/shard_map/all_gather | solution.py:150
  144.6 148.5 %reduce-scatter.21.cloned.1.call-start = ((), (), s32[]{:S(2)}) async-start(), calls=%async_computation.21 | async-start | bytes 1556480 | tf_op jit(solution)/shard_map/reduce_scatter | solution.py:217
  268.6 73.3 %all-gather.49.cloned.1.call-start = ((), (), s32[]{:S(2)}) async-start(), calls=%async_computation.47 | async-start | bytes 1769472 | tf_op jit(solution)/shard_map/all_gather | solution.py:147
  269.4 91.3 %all-gather.31.cloned.1.call-start = ((), (), s32[]{:S(2)}) async-start(), calls=%async_computation.22 | async-start | bytes 1556480 | tf_op jit(solution)/shard_map/all_gather | solution.py:171
  295.5 104.6 %reduce-scatter.23.cloned.1.call-start = ((), (), s32[]{:S(2)}) async-start(), calls=%async_computation.23 | async-start | bytes 1556480 | tf_op jit(solution)/shard_map/reduce_scatter | solution.py:179
  373.9 78.6 %all-gather.51.cloned.1.call-start = ((), (), s32[]{:S(2)}) async-start(), calls=%async_computation.48 | async-start | bytes 2359296 | tf_op jit(solution)/shard_map/all_gather | solution.py:148
  374.6 96.3 %all-gather.33.cloned.1.call-start = ((), (), s32[]{:S(2)}) async-start(), calls=%async_computation.24 | async-start | bytes 1556480 | tf_op jit(solution)/shard_map/all_gather | solution.py:193
  402.4 88.5 %all-gather.35.cloned.1.call-start = ((), (), s32[]{:S(2)}) async-start(), calls=%async_computation.26 | async-start | bytes 1556480 | tf_op jit(solution)/shard_map/all_gather | solution.py:251
  404.1 140.1 %all-gather.53.cloned.1.call-start = ((), (), s32[]{:S(2)}) async-start(), calls=%async_computation.49 | async-start | bytes 2359296 | tf_op jit(solution)/shard_map/all_gather | solution.py:150
  404.7 173.2 %reduce-scatter.27.cloned.1.call-start = ((), (), s32[]{:S(2)}) async-start(), calls=%async_computation.27 | async-start | bytes 1556480 | tf_op jit(solution)/shard_map/reduce_scatter | solution.py:264
  774.3 103.3 %reduce-scatter.45.cloned.1.call-start = ((), (), s32[]{:S(2)}) async-start(), calls=%async_computation.39 | async-start | bytes 1179648 | tf_op jit(solution)/shard_map/reduce_scatter | solution.py:334
  777.4 158.4 %reduce-scatter.43.cloned.1.call-start = ((), (), s32[]{:S(2)}) async-start(), calls=%async_computation.38 | async-start | bytes 1179648 | tf_op jit(solution)/shard_map/reduce_scatter | solution.py:334
  780.4 211.0 %reduce-scatter.37.cloned.1.call-start = ((), (), s32[]{:S(2)}) async-start(), calls=%async_computation.35 | async-start | bytes 36864 | tf_op jit(solution)/shard_map/reduce_scatter | solution.py:336
  781.5 265.5 %reduce-scatter.35.cloned.1.call-start = ((), (), s32[]{:S(2)}) async-start(), calls=%async_computation.34 | async-start | bytes 36864 | tf_op jit(solution)/shard_map/reduce_scatter | solution.py:336
  802.7 335.3 %reduce-scatter.53.cloned.1.call-start = ((), (), s32[]{:S(2)}) async-start(), calls=%async_computation.43 | async-start | bytes 4718592 | tf_op jit(solution)/shard_map/reduce_scatter | solution.py:335
  808.7 421.6 %reduce-scatter.51.cloned.1.call-start = ((), (), s32[]{:S(2)}) async-start(), calls=%async_computation.42 | async-start | bytes 4718592 | tf_op jit(solution)/shard_map/reduce_scatter | solution.py:335
  815.6 506.2 %reduce-scatter.49.cloned.1.call-start = ((), (), s32[]{:S(2)}) async-start(), calls=%async_computation.41 | async-start | bytes 4718592 | tf_op jit(solution)/shard_map/reduce_scatter | solution.py:333
  822.1 591.5 %reduce-scatter.47.cloned.1.call-start = ((), (), s32[]{:S(2)}) async-start(), calls=%async_computation.40 | async-start | bytes 4718592 | tf_op jit(solution)/shard_map/reduce_scatter | solution.py:333
  828.5 663.3 %reduce-scatter.41.cloned.1.call-start = ((), (), s32[]{:S(2)}) async-start(), calls=%async_computation.37 | async-start | bytes 3538944 | tf_op jit(solution)/shard_map/reduce_scatter | solution.py:332
  833.2 736.3 %reduce-scatter.39.cloned.1.call-start = ((), (), s32[]{:S(2)}) async-start(), calls=%async_computation.36 | async-start | bytes 3538944 | tf_op jit(solution)/shard_map/reduce_scatter | solution.py:332
  (99 other events, 2679.2 us)
Sparse Core Ops, SparseCore 0:
  57.3 45.6 all-gather.42
  114.4 24.9 reduce-scatter.18
  142.1 49.3 all-gather.44
  212.6 51.0 all-gather.46
  268.8 24.2 reduce-scatter.20
  295.9 46.0 all-gather.48
  374.0 26.1 reduce-scatter.22
  403.1 49.3 all-gather.50
  493.0 51.0 all-gather.52
  553.5 24.2 reduce-scatter.26
  580.3 26.1 reduce-scatter.24
  651.2 26.1 reduce-scatter.28
  707.7 26.0 reduce-scatter.30
  774.4 26.1 reduce-scatter.32
  804.6 63.9 reduce-scatter.44
  872.8 62.8 reduce-scatter.42
  938.9 52.4 reduce-scatter.36
  994.4 52.5 reduce-scatter.34
  1050.5 87.4 reduce-scatter.52
  1142.1 88.2 reduce-scatter.50
  1234.0 87.7 reduce-scatter.48
  1325.7 87.8 reduce-scatter.46
  1417.2 74.5 reduce-scatter.40
  1495.4 74.0 reduce-scatter.38
  (8 shorter events, 135.1 us)
where the time goes:
time: 1590 us; the launch traced here: 1580 us
  waiting for transfers between devices  1170 us (74%)
  blocking collectives  198 us (12%)
  matrix products  119 us (7%)
  other arithmetic  43.7 us (3%)
  local copies, waits for them, and re-layouts  33.7 us (2%)
  between operations  16.8 us (1%)
    reduce_scatter x2, waiting for transfers between devices, body(): lax.psum_scatter(grad_up_w, 'dp', scatter_dimension=0, tiled=True)  181 us
    reduce_scatter x2, waiting for transfers between devices, body(): lax.psum_scatter(grad_down_w, 'dp', scatter_dimension=1, tiled=True)  171 us
    reduce_scatter x2, waiting for transfers between devices, body(): lax.psum_scatter(grad_qkv_w, 'dp', scatter_dimension=0, tiled=True)  154 us
    reduce_scatter x2, waiting for transfers between devices, body(): lax.psum_scatter(grad_vec, 'dp', scatter_dimension=1, tiled=True)  108 us
    all_gather x2, waiting for transfers between devices, fetch(): lax.all_gather(down_weight[depth], 'dp', axis=1, tiled=True)  102 us
    all_gather x2, blocking collectives, fetch(): lax.all_gather(out_weight[depth], 'dp', axis=1, tiled=True)  59 us
    reduce_scatter x2, waiting for transfers between devices, body(): lax.psum_scatter(grad_out_w, 'dp', scatter_dimension=1, tiled=True)  58.1 us
    all_gather x2, blocking collectives, fetch(): lax.all_gather(up_bias[depth], 'dp', axis=0, tiled=True)  52.4 us
  transfers between devices with their start and end apart: 32, of which 30 were waited for; matrix products, arithmetic and copies ran while one was open for 5% of the time, Pallas kernels for 0%

commit v1 on v0

--- a/solution.py
+++ b/solution.py
@@ -1,9 +1,40 @@
+import functools
 import jax
 import jax.numpy as jnp
 from jax import lax
 from jax.sharding import PartitionSpec as P
+from jax.lax import axis_index, axis_size, ppermute
 
 HEAD_DIM = 64
+
+
+def _shape_rails(message, chip_axis):
+    block_last = axis_size(chip_axis)
+    later = axis_index(chip_axis)
+    all_rows, w_next, r1 = (block_last, later, message.shape[0])
+    by_place = [hop_no * all_rows if no == 0 else hop_no for no, hop_no in enumerate(message.shape)]
+    block_now = lax.dynamic_update_slice_in_dim(
+        jnp.zeros(by_place, message.dtype), message, w_next * r1, axis=0
+    )
+    response = mixed_arr = message
+    for i0 in tuple(range(1, all_rows // 2 + 1)):
+        response = ppermute(
+            response, chip_axis, [(no, (no + 1) % all_rows) for no in range(all_rows)]
+        )
+        block_now = lax.dynamic_update_slice_in_dim(
+            block_now, response, (w_next - i0) % all_rows * r1, axis=0
+        )
+        if 2 * i0 < all_rows:
+            mixed_arr = ppermute(
+                mixed_arr, chip_axis, [(no, (no - 1) % all_rows) for no in range(all_rows)]
+            )
+            block_now = lax.dynamic_update_slice_in_dim(
+                block_now, mixed_arr, (w_next + i0) % all_rows * r1, axis=0
+            )
+    return block_now
+
+
+_arrange_domain = functools.partial(_shape_rails, chip_axis="dp")
 
 
 def layer_norm(values, gain, shift):
@@ -145,7 +176,7 @@
     def fetch(depth):
         return (
             lax.all_gather(qkv_weight[depth], "dp", axis=0, tiled=True),
-            lax.all_gather(up_weight[depth], "dp", axis=0, tiled=True),
+            _arrange_domain(up_weight[depth]),
             lax.all_gather(out_weight[depth], "dp", axis=1, tiled=True),
             lax.all_gather(down_weight[depth], "dp", axis=1, tiled=True),
             lax.all_gather(vectors[depth], "dp", axis=1, tiled=True),

time: 1590 us -> 1510 us (0.950)
  waiting for transfers between devices: 1170 us -> 1030 us
  starting transfers between devices: 2.11 us -> 31.2 us
    all_gather x2, waiting for transfers between devices: 102 us -> 27 us  [fetch(): lax.all_gather(down_weight[depth], 'dp', axis=1, tiled=True)]
    all_gather x2 -> x0, waiting for transfers between devices: 42.2 us -> none  [fetch(): lax.all_gather(up_weight[depth], 'dp', axis=0, tiled=True)]
    ppermute x0 -> x14, waiting for transfers between devices: none -> 38 us  [the longest x6 20.2 us: _shape_rails(): ppermute(mixed_arr, chip_axis, [(no, (no - 1) % all_rows) for no in range...]
    all_gather x2, waiting for transfers between devices: 36.8 us -> 0.01 us  [forward_parts(): lax.all_gather(normed_mid, 'tensor', axis=0, tiled=True)]
    ppermute x0 -> x14, starting transfers between devices: none -> 29.2 us  [the longest x6 17.6 us: _shape_rails(): ppermute(mixed_arr, chip_axis, [(no, (no - 1) % all_rows) for no in range...]
  transfers between devices with their start and end apart: 32 -> 44, of which waited for: 30 -> 34; matrix products, arithmetic and copies ran while one was open for 5% -> 6% of each run, Pallas kernels for 0% -> 0%
where the time goes in v1:
time: 1510 us; the launch traced here: 1500 us
  waiting for transfers between devices  1030 us (68%)
  blocking collectives  207 us (14%)
  matrix products  123 us (8%)
  other arithmetic  45.3 us (3%)
  local copies, waits for them, and re-layouts  44.6 us (3%)
  starting transfers between devices  31.2 us (2%)
  between operations  17.3 us (1%)
    reduce_scatter x2, waiting for transfers between devices, body(): lax.psum_scatter(grad_up_w, 'dp', scatter_dimension=0, tiled=True)  181 us
    reduce_scatter x2, waiting for transfers between devices, body(): lax.psum_scatter(grad_down_w, 'dp', scatter_dimension=1, tiled=True)  171 us
    reduce_scatter x2, waiting for transfers between devices, body(): lax.psum_scatter(grad_qkv_w, 'dp', scatter_dimension=0, tiled=True)  154 us
    reduce_scatter x2, waiting for transfers between devices, body(): lax.psum_scatter(grad_vec, 'dp', scatter_dimension=1, tiled=True)  108 us
    all_gather x2, blocking collectives, fetch(): lax.all_gather(up_bias[depth], 'dp', axis=0, tiled=True)  61.5 us
    all_gather x2, blocking collectives, fetch(): lax.all_gather(out_weight[depth], 'dp', axis=1, tiled=True)  58.9 us
    reduce_scatter x2, waiting for transfers between devices, body(): lax.psum_scatter(grad_out_w, 'dp', scatter_dimension=1, tiled=True)  58.7 us
    reduce_scatter x2, waiting for transfers between devices, forward_parts(): lax.psum_scatter(jnp.einsum('sie,ed->sid', mixed, out_w, preferred_elemen...  51.2 us
  transfers between devices with their start and end apart: 44, of which 34 were waited for; matrix products, arithmetic and copies ran while one was open for 6% of the time, Pallas kernels for 0%

profile of v1, /device:TPU:0, one launch (start us, length us, event | category | flops | bytes accessed | tf_op | source)
XLA Modules:
  0.0 1503.3 jit_solution(15372850661429971435)
XLA Ops:
  14.9 22.4 %all-gather = bf16[1,8,1024]{2,0,1:T(2,128)(2,1)S(1)} all-gather(bf16[1,8,128]{2,0,1:T(2,128)(2,1)S(1)} %get-tuple-element.224), channel_id=2, replica_groups=mesh['dp'=8,'tensor'=4] {'dp'}, dimensions={2}, use_global_device_ids=true | all-gather | bytes 18432 | tf_op jit(solution)/shard_map/all_gather | solution.py:182
  58.1 28.1 %all-gather.2 = bf16[1,256,1024]{2,1,0:T(8,128)(2,1)S(1)} all-gather(bf16[1,256,128]{2,1,0:T(8,128)(2,1)S(1)} %get-tuple-element.201), channel_id=4, replica_groups=mesh['dp'=8,'tensor'=4] {'dp'}, dimensions={2}, use_global_device_ids=true | all-gather | bytes 589824 | tf_op jit(solution)/shard_map/all_gather | solution.py:180
  114.3 25.0 %reduce-scatter.19.cloned.1.call-done = bf16[152,1,1024]{2,0,1:T(8,128)(2,1)} async-done(((bf16[608,1,1024]{2,0,1:T(8,128)(2,1)}), bf16[152,1,1024]{2,0,1:T(8,128)(2,1)}) %reduce-scatter.19.cloned.1.call-update) | async-done | bytes 311312 | tf_op jit(solution)/shard_map/reduce_scatter | solution.py:210
  150.1 30.7 %all-gather.3 = bf16[1,4096]{1,0:T(2,128)(2,1)S(1)} all-gather(bf16[1,512]{1,0:T(2,128)(2,1)S(1)} %get-tuple-element.227), channel_id=5, replica_groups=mesh['dp'=8,'tensor'=4] {'dp'}, dimensions={1}, use_global_device_ids=true | all-gather | bytes 9216 | tf_op jit(solution)/shard_map/all_gather | solution.py:183
  234.0 23.9 %reduce-scatter.21.cloned.1.call-done = bf16[152,1,1024]{2,0,1:T(8,128)(2,1)} async-done(((bf16[608,1,1024]{2,0,1:T(8,128)(2,1)}), bf16[152,1,1024]{2,0,1:T(8,128)(2,1)}) %reduce-scatter.21.cloned.1.call-update) | async-done | bytes 311312 | tf_op jit(solution)/shard_map/reduce_scatter | solution.py:248
  260.4 30.8 %all-gather.7 = bf16[1,256,1024]{2,1,0:T(8,128)(2,1)} all-gather(bf16[1,256,128]{2,1,0:T(8,128)(2,1)S(1)} %get-tuple-element.200), channel_id=9, replica_groups=mesh['dp'=8,'tensor'=4] {'dp'}, dimensions={2}, use_global_device_ids=true | all-gather | bytes 589824 | tf_op jit(solution)/shard_map/all_gather | solution.py:180
  306.6 18.8 %all-gather.27.cloned.1.call-done = bf16[608,1,1024]{2,0,1:T(8,128)(2,1)} async-done(((bf16[152,1,1024]{2,0,1:T(8,128)(2,1)}), bf16[608,1,1024]{2,0,1:T(8,128)(2,1)}) %all-gather.27.cloned.1.call-update) | async-done | bytes 1245200 | tf_op jit(solution)/shard_map/all_gather | solution.py:202
  338.5 26.2 %reduce-scatter.23.cloned.1.call-done = bf16[152,1,1024]{2,0,1:T(8,128)(2,1)} async-done(((bf16[608,1,1024]{2,0,1:T(8,128)(2,1)}), bf16[152,1,1024]{2,0,1:T(8,128)(2,1)}) %reduce-scatter.23.cloned.1.call-update) | async-done | bytes 311312 | tf_op jit(solution)/shard_map/reduce_scatter | solution.py:210
  375.0 30.8 %all-gather.8 = bf16[1,4096]{1,0:T(2,128)(2,1)S(1)} all-gather(bf16[1,512]{1,0:T(2,128)(2,1)S(1)} %get-tuple-element.226), channel_id=10, replica_groups=mesh['dp'=8,'tensor'=4] {'dp'}, dimensions={1}, use_global_device_ids=true | all-gather | bytes 9216 | tf_op jit(solution)/shard_map/all_gather | solution.py:183
  445.4 21.4 %all-gather.45.cloned.1.call-done = bf16[1,1024,1024]{2,1,0:T(8,128)(2,1)} async-done(((bf16[1,1024,128]{2,1,0:T(8,128)(2,1)}), bf16[1,1024,1024]{2,1,0:T(8,128)(2,1)}) %all-gather.45.cloned.1.call-update) | async-done | bytes 2097168 | tf_op jit(solution)/shard_map/all_gather | solution.py:181
  483.1 18.9 %reduce-scatter.27.cloned.1.call-done = bf16[152,1,1024]{2,0,1:T(8,128)(2,1)} async-done(((bf16[608,1,1024]{2,0,1:T(8,128)(2,1)}), bf16[152,1,1024]{2,0,1:T(8,128)(2,1)}) %reduce-scatter.27.cloned.1.call-update) | async-done | bytes 311312 | tf_op jit(solution)/shard_map/reduce_scatter | solution.py:295
  504.0 26.7 %reduce-scatter.25.cloned.1.call-done = bf16[152,1,1024]{2,0,1:T(8,128)(2,1)} async-done(((bf16[608,1,1024]{2,0,1:T(8,128)(2,1)}), bf16[152,1,1024]{2,0,1:T(8,128)(2,1)}) %reduce-scatter.25.cloned.1.call-update) | async-done | bytes 311312 | tf_op jit(solution)/shard_map/reduce_scatter | solution.py:248
  575.3 26.2 %reduce-scatter.29.cloned.1.call-done = bf16[152,1,1024]{2,0,1:T(8,128)(2,1)} async-done(((bf16[608,1,1024]{2,0,1:T(8,128)(2,1)}), bf16[152,1,1024]{2,0,1:T(8,128)(2,1)}) %reduce-scatter.29.cloned.1.call-update) | async-done | bytes 311312 | tf_op jit(solution)/shard_map/reduce_scatter | solution.py:325
  632.4 26.2 %reduce-scatter.31.cloned.1.call-done = bf16[152,1,1024]{2,0,1:T(8,128)(2,1)} async-done(((bf16[608,1,1024]{2,0,1:T(8,128)(2,1)}), bf16[152,1,1024]{2,0,1:T(8,128)(2,1)}) %reduce-scatter.31.cloned.1.call-update) | async-done | bytes 311312 | tf_op jit(solution)/shard_map/reduce_scatter | solution.py:295
  764.7 37.1 %all-reduce.2 = (f32[4096]{0:T(1024)S(1)}, f32[4096]{0:T(1024)S(1)}) all-reduce(f32[4096]{0:T(1024)S(1)} %dynamic_update_slice.112, f32[4096]{0:T(1024)S(1)} %dynamic_update_slice.111), channel_id=29, replica_groups=mesh['dp'=8,'tensor'=4] {'dp'}, use_global_device_ids=true, to_apply=%region_56.57.clone | all-reduce | flops 8192 | bytes 65536
  802.0 58.7 %reduce-scatter.43.cloned.1.call-done = f32[256,128]{1,0:T(8,128)} async-done(((f32[256,1024]{1,0:T(8,128)}), f32[256,128]{1,0:T(8,128)}) %reduce-scatter.43.cloned.1.call-update) | async-done | bytes 131088 | tf_op jit(solution)/shard_map/reduce_scatter | solution.py:365
  864.1 52.3 %reduce-scatter.37.cloned.1.call-done = f32[8,128]{1,0:T(8,128)} async-done(((f32[8,1024]{1,0:T(8,128)}), f32[8,128]{1,0:T(8,128)}) %reduce-scatter.37.cloned.1.call-update) | async-done | bytes 4112 | tf_op jit(solution)/shard_map/reduce_scatter | solution.py:367
  916.4 55.5 %reduce-scatter.35.cloned.1.call-done = f32[8,128]{1,0:T(8,128)} async-done(((f32[8,1024]{1,0:T(8,128)}), f32[8,128]{1,0:T(8,128)}) %reduce-scatter.35.cloned.1.call-update) | async-done | bytes 4112 | tf_op jit(solution)/shard_map/reduce_scatter | solution.py:367
  983.9 79.1 %reduce-scatter.53.cloned.1.call-done = f32[1024,128]{1,0:T(8,128)} async-done(((f32[1024,1024]{1,0:T(8,128)}), f32[1024,128]{1,0:T(8,128)}) %reduce-scatter.53.cloned.1.call-update) | async-done | bytes 524304 | tf_op jit(solution)/shard_map/reduce_scatter | solution.py:366
  1063.0 92.2 %reduce-scatter.51.cloned.1.call-done = f32[1024,128]{1,0:T(8,128)} async-done(((f32[1024,1024]{1,0:T(8,128)}), f32[1024,128]{1,0:T(8,128)}) %reduce-scatter.51.cloned.1.call-update) | async-done | bytes 524304 | tf_op jit(solution)/shard_map/reduce_scatter | solution.py:366
  1157.5 88.9 %reduce-scatter.49.cloned.1.call-done = f32[128,1024]{1,0:T(8,128)} async-done(((f32[1024,1024]{1,0:T(8,128)}), f32[128,1024]{1,0:T(8,128)}) %reduce-scatter.49.cloned.1.call-update) | async-done | bytes 524304 | tf_op jit(solution)/shard_map/reduce_scatter | solution.py:364
  1246.4 91.8 %reduce-scatter.47.cloned.1.call-done = f32[128,1024]{1,0:T(8,128)} async-done(((f32[1024,1024]{1,0:T(8,128)}), f32[128,1024]{1,0:T(8,128)}) %reduce-scatter.47.cloned.1.call-update) | async-done | bytes 524304 | tf_op jit(solution)/shard_map/reduce_scatter | solution.py:364
  1340.4 76.0 %reduce-scatter.41.cloned.1.call-done = f32[128,3,256]{2,0,1:T(8,128)} async-done(((f32[1024,3,256]{2,0,1:T(8,128)}), f32[128,3,256]{2,0,1:T(8,128)}) %reduce-scatter.41.cloned.1.call-update) | async-done | bytes 393232 | tf_op jit(solution)/shard_map/reduce_scatter | solution.py:363
  1416.4 77.6 %reduce-scatter.39.cloned.1.call-done = f32[128,3,256]{2,0,1:T(8,128)} async-done(((f32[1024,3,256]{2,0,1:T(8,128)}), f32[128,3,256]{2,0,1:T(8,128)}) %reduce-scatter.39.cloned.1.call-update) | async-done | bytes 393232 | tf_op jit(solution)/shard_map/reduce_scatter | solution.py:363
  (433 shorter events, 420.6 us)
Async XLA Ops:
  7.2 79.0 %all-gather.23.cloned.1.call-start = ((), (), s32[]{:S(2)}) async-start(), calls=%async_computation.18 | async-start | bytes 1556480 | tf_op jit(solution)/shard_map/all_gather | solution.py:202
  41.2 98.1 %reduce-scatter.19.cloned.1.call-start = ((), (), s32[]{:S(2)}) async-start(), calls=%async_computation.19 | async-start | bytes 1556480 | tf_op jit(solution)/shard_map/reduce_scatter | solution.py:210
  114.3 103.6 %all-gather.25.cloned.1.call-start = ((), (), s32[]{:S(2)}) async-start(), calls=%async_computation.20 | async-start | bytes 1556480 | tf_op jit(solution)/shard_map/all_gather | solution.py:224
  143.6 84.7 %all-gather.41.cloned.1.call-start = ((), (), s32[]{:S(2)}) async-start(), calls=%async_computation.45 | async-start | bytes 2359296 | tf_op jit(solution)/shard_map/all_gather | solution.py:181
  144.5 113.5 %reduce-scatter.21.cloned.1.call-start = ((), (), s32[]{:S(2)}) async-start(), calls=%async_computation.21 | async-start | bytes 1556480 | tf_op jit(solution)/shard_map/reduce_scatter | solution.py:248
  233.2 73.4 %all-gather.43.cloned.1.call-start = ((), (), s32[]{:S(2)}) async-start(), calls=%async_computation.46 | async-start | bytes 1769472 | tf_op jit(solution)/shard_map/all_gather | solution.py:178
  234.0 91.4 %all-gather.27.cloned.1.call-start = ((), (), s32[]{:S(2)}) async-start(), calls=%async_computation.22 | async-start | bytes 1556480 | tf_op jit(solution)/shard_map/all_gather | solution.py:202
  260.4 104.3 %reduce-scatter.23.cloned.1.call-start = ((), (), s32[]{:S(2)}) async-start(), calls=%async_computation.23 | async-start | bytes 1556480 | tf_op jit(solution)/shard_map/reduce_scatter | solution.py:210
  338.4 102.2 %all-gather.29.cloned.1.call-start = ((), (), s32[]{:S(2)}) async-start(), calls=%async_computation.24 | async-start | bytes 1556480 | tf_op jit(solution)/shard_map/all_gather | solution.py:224
  367.0 78.4 %all-gather.31.cloned.1.call-start = ((), (), s32[]{:S(2)}) async-start(), calls=%async_computation.26 | async-start | bytes 1556480 | tf_op jit(solution)/shard_map/all_gather | solution.py:282
  369.6 97.3 %all-gather.45.cloned.1.call-start = ((), (), s32[]{:S(2)}) async-start(), calls=%async_computation.47 | async-start | bytes 2359296 | tf_op jit(solution)/shard_map/all_gather | solution.py:181
  370.2 131.8 %reduce-scatter.27.cloned.1.call-start = ((), (), s32[]{:S(2)}) async-start(), calls=%async_computation.27 | async-start | bytes 1556480 | tf_op jit(solution)/shard_map/reduce_scatter | solution.py:295
  483.1 70.0 %all-gather.33.cloned.1.call-start = ((), (), s32[]{:S(2)}) async-start(), calls=%async_computation.28 | async-start | bytes 1556480 | tf_op jit(solution)/shard_map/all_gather | solution.py:308
  535.1 66.4 %reduce-scatter.29.cloned.1.call-start = ((), (), s32[]{:S(2)}) async-start(), calls=%async_computation.29 | async-start | bytes 1556480 | tf_op jit(solution)/shard_map/reduce_scatter | solution.py:325
  699.0 103.0 %reduce-scatter.45.cloned.1.call-start = ((), (), s32[]{:S(2)}) async-start(), calls=%async_computation.39 | async-start | bytes 1179648 | tf_op jit(solution)/shard_map/reduce_scatter | solution.py:365
  702.0 158.7 %reduce-scatter.43.cloned.1.call-start = ((), (), s32[]{:S(2)}) async-start(), calls=%async_computation.38 | async-start | bytes 1179648 | tf_op jit(solution)/shard_map/reduce_scatter | solution.py:365
  705.1 211.3 %reduce-scatter.37.cloned.1.call-start = ((), (), s32[]{:S(2)}) async-start(), calls=%async_computation.35 | async-start | bytes 36864 | tf_op jit(solution)/shard_map/reduce_scatter | solution.py:367
  707.1 264.9 %reduce-scatter.35.cloned.1.call-start = ((), (), s32[]{:S(2)}) async-start(), calls=%async_computation.34 | async-start | bytes 36864 | tf_op jit(solution)/shard_map/reduce_scatter | solution.py:367
  727.4 335.6 %reduce-scatter.53.cloned.1.call-start = ((), (), s32[]{:S(2)}) async-start(), calls=%async_computation.43 | async-start | bytes 4718592 | tf_op jit(solution)/shard_map/reduce_scatter | solution.py:366
  733.4 421.8 %reduce-scatter.51.cloned.1.call-start = ((), (), s32[]{:S(2)}) async-start(), calls=%async_computation.42 | async-start | bytes 4718592 | tf_op jit(solution)/shard_map/reduce_scatter | solution.py:366
  740.1 506.3 %reduce-scatter.49.cloned.1.call-start = ((), (), s32[]{:S(2)}) async-start(), calls=%async_computation.41 | async-start | bytes 4718592 | tf_op jit(solution)/shard_map/reduce_scatter | solution.py:364
  745.7 592.5 %reduce-scatter.47.cloned.1.call-start = ((), (), s32[]{:S(2)}) async-start(), calls=%async_computation.40 | async-start | bytes 4718592 | tf_op jit(solution)/shard_map/reduce_scatter | solution.py:364
  751.2 665.2 %reduce-scatter.41.cloned.1.call-start = ((), (), s32[]{:S(2)}) async-start(), calls=%async_computation.37 | async-start | bytes 3538944 | tf_op jit(solution)/shard_map/reduce_scatter | solution.py:363
  756.7 737.3 %reduce-scatter.39.cloned.1.call-start = ((), (), s32[]{:S(2)}) async-start(), calls=%async_computation.36 | async-start | bytes 3538944 | tf_op jit(solution)/shard_map/reduce_scatter | solution.py:363
  (103 other events, 2509.7 us)
Sparse Core Ops, SparseCore 0:
  57.3 45.5 all-gather.38
  114.4 24.8 reduce-scatter.18
  143.7 17.8 all-gather.24
  164.3 63.9 all-gather.40
  233.3 24.5 reduce-scatter.20
  260.7 45.8 all-gather.42
  338.6 26.1 reduce-scatter.22
  407.2 59.6 all-gather.44
  477.7 24.2 reduce-scatter.26
  504.5 26.1 reduce-scatter.24
  575.4 26.1 reduce-scatter.28
  632.4 26.1 reduce-scatter.30
  663.4 17.8 all-gather.36
  699.1 26.1 reduce-scatter.32
  729.3 63.9 reduce-scatter.44
  797.7 62.9 reduce-scatter.42
  863.8 52.5 reduce-scatter.36
  919.4 52.5 reduce-scatter.34
  975.6 87.4 reduce-scatter.52
  1066.9 88.2 reduce-scatter.50
  1158.7 87.6 reduce-scatter.48
  1250.4 87.6 reduce-scatter.46
  1341.8 74.6 reduce-scatter.40
  1419.9 74.1 reduce-scatter.38
  (6 shorter events, 102.6 us)
